TPU v7x, 32 devices: a whole 2x2x4 slice. The times are simulated.
32 devices in a mesh: wide: 4 (over z), narrow: 8 (over y, x, core).
Axes of the slice: x: 2, y: 2, z: 4, core: 2. Of those that a mesh axis runs over, the one named last changes fastest.
Arguments:
- saved_inputs: bfloat16 [1024, 5120], P('wide', 'narrow'), may hold values from -6 to 6
- out_grads: bfloat16 [1024, 5120], P('wide', 'narrow'), may hold values from -48 to 48
- seq_ids: int32 [1024], P('wide'), may hold values from 0 to 7, as said below
- seq_counts: int32 [8], P('wide'), may hold values from 64 to 192, as said below
- basis_in: bfloat16 [5120, 5120], P('narrow'), may hold values from -0.078125 to 0.078125
- basis_out: bfloat16 [5120, 5120], P('narrow'), may hold values from -0.078125 to 0.078125
- query_rotated: bfloat16 [5120, 5120], P('narrow', 'wide'), may hold values from -6 to 6
- damping: float32 [], replicated, may hold values from 0.05 to 0.5
Outputs:
- eigenvalues: float32 [5120, 5120], P('narrow', 'wide')
- preconditioned: float32 [5120, 5120], P('narrow', 'wide')
Inputs may be any that keep to these rules, and one draw needn't show every extreme that they name: seq_ids names for each token its sequence; the 256 tokens of block w of the token axis belong to the sequences 2 * w to 2 * w + 1, each having at least one token. seq_counts[s] is the number of tokens whose seq_ids equal s.
All inputs are finite; a program needn't handle non-finite values.
Results may differ from a plain program's by a relative error of at most 0.01.
Values may be sent and summed in bfloat16 or wider, within the bound.
No kernel may reach another device: no remote copies, remote signals or barrier semaphores. Data moves between devices by JAX's collectives and lax.ppermute only.
A program may use at most 128 MiB of HBM per device.

v0:
```python
import jax
import jax.numpy as jnp
from jax import lax
from jax.sharding import PartitionSpec as P


def shards(
    saved_inputs, out_grads, seq_ids, seq_counts, basis_in, basis_out, query_rotated, damping
):
    part_in = jnp.dot(saved_inputs, basis_in, preferred_element_type=jnp.float32)
    part_grad = jnp.dot(out_grads, basis_out, preferred_element_type=jnp.float32)
    rot_in = lax.psum(part_in, "narrow").astype(jnp.bfloat16)
    rot_grad = lax.psum_scatter(part_grad, "narrow", scatter_dimension=1, tiled=True).astype(
        jnp.bfloat16
    )
    seq_local = seq_counts.shape[0]
    tok_local = seq_ids.shape[0]
    offset = lax.axis_index("wide") * seq_local
    member = seq_ids[None, :] - offset == jnp.arange(seq_local, dtype=jnp.int32)[:, None]
    weight = (
        jnp.where(member, 1.0, 0.0).astype(jnp.float32) / seq_counts.astype(jnp.float32)[:, None]
    )
    weighted = (rot_grad.astype(jnp.float32)[None, :, :] * weight[:, :, None]).astype(jnp.bfloat16)
    total_seqs = seq_local * lax.axis_size("wide")
    groups = lax.axis_size("wide")
    all_weighted = lax.all_gather(weighted, "wide", axis=0, tiled=True)
    all_weighted = all_weighted.reshape(groups, seq_local, tok_local, all_weighted.shape[2])
    column_rows = lax.all_to_all(rot_in, "wide", split_axis=1, concat_axis=0, tiled=True)
    column_rows = column_rows.reshape(groups, tok_local, column_rows.shape[1])
    per_seq = jnp.einsum(
        "gsti,gtj->gsij", all_weighted, column_rows, preferred_element_type=jnp.float32
    )
    eigenvalues = jnp.sum(per_seq * per_seq, axis=(0, 1)) / total_seqs
    scaled = (query_rotated.astype(jnp.float32) / (eigenvalues + damping)).astype(jnp.bfloat16)
    width = query_rotated.shape[1]
    in_columns = lax.dynamic_slice_in_dim(basis_in, lax.axis_index("wide") * width, width, 1)
    all_scaled, all_columns = (
        lax.all_gather(scaled, "narrow", axis=0, tiled=True),
        lax.all_gather(in_columns, "narrow", axis=0, tiled=True),
    )
    middle = jnp.dot(basis_out, all_scaled, preferred_element_type=jnp.float32).astype(jnp.bfloat16)
    partial_back = lax.dot_general(
        middle, all_columns, (((1,), (1,)), ((), ())), preferred_element_type=jnp.float32
    )
    preconditioned = lax.psum_scatter(partial_back, "wide", scatter_dimension=1, tiled=True)
    return (eigenvalues, preconditioned)


def solution(mesh):
    return jax.shard_map(
        shards,
        mesh=mesh,
        in_specs=(
            P("wide", "narrow"),
            P("wide", "narrow"),
            P("wide"),
            P("wide"),
            P("narrow", None),
            P("narrow", None),
            P("narrow", "wide"),
            P(),
        ),
        out_specs=(P("narrow", "wide"), P("narrow", "wide")),
        check_vma=False,
    )
```

profile of v0, /device:TPU:0, one launch (start us, length us, event | category | flops | bytes accessed | tf_op | source)
XLA Modules:
  0.0 662.8 jit_solution(4311589889708317204)
XLA Ops:
  7.2 0.0 reduce-scatter.3.cloned.1.call-start
  7.2 0.9 copy-done
  8.1 7.4 %fusion.3 = f32[256,5120]{1,0:T(8,128)} fusion(bf16[256,640]{1,0:T(8,128)(2,1)S(1)} %copy-done, bf16[640,5120]{1,0:T(8,128)(2,1)} %param.13), kind=kOutput, calls=%fused_computation.13 | convolution fusion | flops 1677721600 | bytes 12124160 | tf_op jit(solution)/shard_map/dot_general | solution.py:11
  15.5 0.0 reduce-scatter.3.cloned.1.call-update
  15.5 0.9 copy-done.3
  16.5 7.4 %fusion.4 = f32[256,5120]{1,0:T(8,128)} fusion(bf16[256,640]{1,0:T(8,128)(2,1)S(1)} %copy-done.3, bf16[640,5120]{1,0:T(8,128)(2,1)} %param.12), kind=kOutput, calls=%fused_computation.14 | convolution fusion | flops 1677721600 | bytes 12124160 | tf_op jit(solution)/shard_map/dot_general | solution.py:10
  23.9 130.5 %all-reduce.1 = bf16[256,5120]{1,0:T(8,128)(2,1)S(1)} all-reduce(f32[256,5120]{1,0:T(8,128)} %fusion.4), channel_id=1, replica_groups=mesh['wide'=4,'narrow'=8] {'narrow'}, use_global_device_ids=true, to_apply=%region_1.0 | all-reduce | flops 1310720 | bytes 7864320 | tf_op jit(solution)/shard_map/psum | solution.py:12
  154.3 1.7 copy.17
  156.0 5.1 all-to-all-start
  161.1 0.1 fusion.2
  161.2 1.1 convert_convert_fusion
  162.3 1.0 multiply_convert_fusion
  163.3 0.0 all-gather.6.cloned.1.call-start
  164.0 97.9 %all-to-all-done = bf16[256,4,1280]{2,0,1:T(8,128)(2,1)S(1)} async-done(((bf16[256,4,1280]{2,0,1:T(8,128)(2,1)}), bf16[256,4,1280]{2,0,1:T(8,128)(2,1)S(1)}, u32[]{:S(2)}, u32[]{:S(2)}) %all-to-all-start) | async-done | bytes 2621472 | tf_op jit(solution)/shard_map/all_to_all | solution.py:28
  261.9 6.7 %multiply_reduce_fusion = f32[640,1280]{1,0:T(8,128)S(1)} fusion(bf16[4,2,256,640]{3,2,1,0:T(8,128)(2,1)} %bitcast.30, bf16[256,4,1280]{2,0,1:T(8,128)(2,1)S(1)} %all-to-all-done), kind=kOutput, calls=%fused_computation | convolution fusion | flops 3367731200 | bytes 8519680 | tf_op jit(solution)/shard_map/gsti,gtj->gsij/dot_general | solution.py:30
  268.6 2.9 divide_convert_fusion
  271.5 0.0 all-gather.8.cloned.1.call-start
  271.5 2.7 constant_dynamic-slice_fusion
  274.3 0.2 reduce-scatter.5.cloned.1.call-start
  274.5 70.8 %all-gather.6.cloned.1.call-done = bf16[5120,1280]{1,0:T(8,128)(2,1)} async-done(((bf16[640,1280]{1,0:T(8,128)(2,1)}), bf16[5120,1280]{1,0:T(8,128)(2,1)}) %all-gather.6.cloned.1.call-update) | async-done | bytes 13107216 | tf_op jit(solution)/shard_map/all_gather | solution.py:38
  345.3 15.3 %convolution_convert_fusion.clone.4 = bf16[1280,640]{1,0:T(8,128)(2,1)S(1)} fusion(bf16[5120,1280]{1,0:T(8,128)(2,1)} %all-gather.6.cloned.1.call-done, bf16[640,5120]{1,0:T(8,128)(2,1)} %param.13), kind=kOutput, calls=%fused_computation.2.clone.clone.clone.1 | convolution fusion | flops 8389427200 | bytes 21299200 | tf_op jit(solution)/shard_map/dot_general | solution.py:41
  360.6 60.7 %all-gather.8.cloned.1.call-done = bf16[5120,1280]{1,0:T(8,128)(2,1)} async-done(((bf16[640,1280]{1,0:T(8,128)(2,1)}), bf16[5120,1280]{1,0:T(8,128)(2,1)}) %all-gather.8.cloned.1.call-update) | async-done | bytes 13107216 | tf_op jit(solution)/shard_map/all_gather | solution.py:39
  421.2 14.5 %fusion.1 = f32[640,5120]{1,0:T(8,128)} fusion(bf16[5120,1280]{1,0:T(8,128)(2,1)} %all-gather.8.cloned.1.call-done, bf16[1280,640]{1,0:T(8,128)(2,1)S(1)} %convolution_convert_fusion.clone.4), kind=kOutput, calls=%fused_computation.5 | convolution fusion | flops 8388608000 | bytes 27852800 | tf_op jit(solution)/shard_map/dot_general | solution.py:42
  435.8 220.5 %reduce-scatter.5.cloned.1.call-done = f32[640,1280]{1,0:T(8,128)} async-done(((f32[640,5120]{1,0:T(8,128)}), f32[640,1280]{1,0:T(8,128)}) %reduce-scatter.5.cloned.1.call-update) | async-done | bytes 3276816 | tf_op jit(solution)/shard_map/reduce_scatter | solution.py:45
  (19 shorter events, 0.1 us)
Async XLA Ops:
  7.2 1.0 copy-start
  7.2 154.0 %reduce-scatter.3.cloned.1.call-start = ((), (), s32[]{:S(2)}) async-start(), calls=%async_computation.3 | async-start | bytes 5898240 | tf_op jit(solution)/shard_map/reduce_scatter | solution.py:13
  15.5 1.0 copy-start.3
  156.0 5.1 copy-start.5
  156.0 5.1 copy-start.4
  156.0 105.9 %all-to-all-start = ((bf16[256,4,1280]{2,0,1:T(8,128)(2,1)}), bf16[256,4,1280]{2,0,1:T(8,128)(2,1)S(1)}, u32[]{:S(2)}, u32[]{:S(2)}) async-start(bf16[256,4,1280]{2,0,1:T(8,128)(2,1)} %bitcast.28), calls=%async_computation.1 | async-start | bytes 5242880 | tf_op jit(solution)/shard_map/all_to_all | solution.py:28
  161.1 100.8 %all-gather.4.cloned.1.call-start = ((), (), s32[]{:S(2)}) async-start(), calls=%async_computation.4 | async-start | bytes 3276800 | tf_op jit(solution)/shard_map/all_gather | solution.py:26
  163.3 181.9 %all-gather.6.cloned.1.call-start = ((), (), s32[]{:S(2)}) async-start(), calls=%async_computation.5 | async-start | bytes 14745600 | tf_op jit(solution)/shard_map/all_gather | solution.py:38
  261.9 6.7 %copy-start.2 = (bf16[640,1280]{1,0:T(8,128)(2,1)S(1)}, bf16[640,1280]{1,0:T(8,128)(2,1)}, u32[]{:S(2)}) copy-start(bf16[640,1280]{1,0:T(8,128)(2,1)} %param.14) | copy-start | bytes 4915204
  271.5 149.8 %all-gather.8.cloned.1.call-start = ((), (), s32[]{:S(2)}) async-start(), calls=%async_computation.6 | async-start | bytes 14745600 | tf_op jit(solution)/shard_map/all_gather | solution.py:39
  274.3 382.0 %reduce-scatter.5.cloned.1.call-start = ((), (), s32[]{:S(2)}) async-start(), calls=%async_computation.7 | async-start | bytes 16384000 | tf_op jit(solution)/shard_map/reduce_scatter | solution.py:45
  435.8 220.5 %copy-start.1 = (bf16[256,640]{1,0:T(8,128)(2,1)S(1)}, bf16[256,640]{1,0:T(8,128)(2,1)}, u32[]{:S(2)}) copy-start(bf16[256,640]{1,0:T(8,128)(2,1)} %param.9) | copy-start | bytes 983044
Sparse Core Ops, SparseCore 0:
  15.7 80.4 reduce-scatter.2
  164.0 92.1 all-gather.3
  271.6 73.6 all-gather.5
  347.0 74.1 all-gather.7
  435.9 220.3 reduce-scatter.4
where the time goes:
time: 663 us
  waiting for transfers between devices  450 us (68%)
  blocking collectives  130 us (20%)
  matrix products  51.3 us (8%)
  between operations  14.5 us (2%)
    reduce_scatter x1, waiting for transfers between devices, shards(): lax.psum_scatter(partial_back, 'wide', scatter_dimension=1, tiled=True)  220 us
    psum x1, blocking collectives, shards(): rot_in = lax.psum(part_in, 'narrow').astype(jnp.bfloat16)  130 us
    all_to_all x1, waiting for transfers between devices, shards(): lax.all_to_all(rot_in, 'wide', split_axis=1, concat_axis=0, tiled=True)  97.9 us
    all_gather x1, waiting for transfers between devices, shards(): lax.all_gather(scaled, 'narrow', axis=0, tiled=True)  70.8 us
    all_gather x1, waiting for transfers between devices, shards(): lax.all_gather(in_columns, 'narrow', axis=0, tiled=True)  60.7 us
    dot_general x1, matrix products, shards(): jnp.dot(basis_out, all_scaled, preferred_element_type=jnp.float32)  15.3 us
    dot_general x1, matrix products, shards(): lax.dot_general(middle, all_columns, (((1,), (1,)), ((), ())), preferred_...  14.5 us
  transfers between devices with their start and end apart: 6, of which 4 were waited for; matrix products, arithmetic and copies ran while one was open for 4% of the time, Pallas kernels for 0%

commit v1 on v0

--- a/solution.py
+++ b/solution.py
@@ -1,7 +1,17 @@
+import functools
 import jax
 import jax.numpy as jnp
 from jax import lax
 from jax.sharding import PartitionSpec as P
+
+
+def task_point(values, chip_axis):
+    piece_now = jnp.split(values, lax.axis_size(chip_axis), axis=1)
+    everything = jnp.stack(piece_now, axis=0)
+    return jnp.concatenate(lax.all_to_all(everything, chip_axis, 0, 0), axis=0)
+
+
+arrange_tokens_on = functools.partial(task_point, chip_axis="wide")
 
 
 def shards(
@@ -25,7 +35,7 @@
     groups = lax.axis_size("wide")
     all_weighted = lax.all_gather(weighted, "wide", axis=0, tiled=True)
     all_weighted = all_weighted.reshape(groups, seq_local, tok_local, all_weighted.shape[2])
-    column_rows = lax.all_to_all(rot_in, "wide", split_axis=1, concat_axis=0, tiled=True)
+    column_rows = arrange_tokens_on(rot_in)
     column_rows = column_rows.reshape(groups, tok_local, column_rows.shape[1])
     per_seq = jnp.einsum(
         "gsti,gtj->gsij", all_weighted, column_rows, preferred_element_type=jnp.float32

time: 663 us -> 664 us (level)
  no operation moved by 1% of the time
where the time goes in v1:
time: 664 us; the launch traced here: 663 us
  waiting for transfers between devices  450 us (68%)
  blocking collectives  130 us (20%)
  matrix products  51.5 us (8%)
  between operations  14.5 us (2%)
  other arithmetic  6.88 us (1%)
    reduce_scatter x1, waiting for transfers between devices, shards(): lax.psum_scatter(partial_back, 'wide', scatter_dimension=1, tiled=True)  220 us
    psum x1, blocking collectives, shards(): rot_in = lax.psum(part_in, 'narrow').astype(jnp.bfloat16)  130 us
    all_to_all x1, waiting for transfers between devices, task_point(): return jnp.concatenate(lax.all_to_all(everything, chip_axis, 0, 0), axis=0)  97.9 us
    all_gather x1, waiting for transfers between devices, shards(): lax.all_gather(scaled, 'narrow', axis=0, tiled=True)  70.8 us
    all_gather x1, waiting for transfers between devices, shards(): lax.all_gather(in_columns, 'narrow', axis=0, tiled=True)  60.4 us
    dot_general x1, matrix products, shards(): jnp.dot(basis_out, all_scaled, preferred_element_type=jnp.float32)  15.5 us
    dot_general x1, matrix products, shards(): lax.dot_general(middle, all_columns, (((1,), (1,)), ((), ())), preferred_...  14.5 us
  transfers between devices with their start and end apart: 6, of which 4 were waited for; matrix products, arithmetic and copies ran while one was open for 4% of the time, Pallas kernels for 0%

profile of v1, /device:TPU:0, one launch (start us, length us, event | category | flops | bytes accessed | tf_op | source)
XLA Modules:
  0.0 663.1 jit_solution(15507166695013119454)
XLA Ops:
  7.2 0.0 reduce-scatter.3.cloned.1.call-start
  7.2 0.9 copy-done
  8.1 7.4 %fusion.3 = f32[256,5120]{1,0:T(8,128)} fusion(bf16[256,640]{1,0:T(8,128)(2,1)S(1)} %copy-done, bf16[640,5120]{1,0:T(8,128)(2,1)} %param.13), kind=kOutput, calls=%fused_computation.17 | convolution fusion | flops 1677721600 | bytes 12124160 | tf_op jit(solution)/shard_map/dot_general | solution.py:21
  15.5 0.9 copy-done.3
  16.5 7.4 %fusion.4 = f32[256,5120]{1,0:T(8,128)} fusion(bf16[256,640]{1,0:T(8,128)(2,1)S(1)} %copy-done.3, bf16[640,5120]{1,0:T(8,128)(2,1)} %param.12), kind=kOutput, calls=%fused_computation.18 | convolution fusion | flops 1677721600 | bytes 12124160 | tf_op jit(solution)/shard_map/dot_general | solution.py:20
  23.9 130.5 %all-reduce.1 = bf16[256,5120]{1,0:T(8,128)(2,1)S(1)} all-reduce(f32[256,5120]{1,0:T(8,128)} %fusion.4), channel_id=1, replica_groups=mesh['wide'=4,'narrow'=8] {'narrow'}, use_global_device_ids=true, to_apply=%region_1.0 | all-reduce | flops 1310720 | bytes 7864320 | tf_op jit(solution)/shard_map/psum | solution.py:22
  154.3 0.2 slice_bitcast_fusion.3
  154.5 1.8 pad_maximum_fusion
  156.3 5.1 all-to-all-start
  161.4 0.1 fusion.2
  161.5 1.1 convert_convert_fusion
  162.7 1.0 multiply_convert_fusion
  163.7 0.0 all-gather.6.cloned.1.call-start
  164.4 97.9 %all-to-all-done = bf16[4,256,1280]{2,1,0:T(8,128)(2,1)S(1)} async-done(((bf16[4,256,1280]{2,1,0:T(8,128)(2,1)}), bf16[4,256,1280]{2,1,0:T(8,128)(2,1)S(1)}, u32[]{:S(2)}, u32[]{:S(2)}) %all-to-all-start) | async-done | bytes 2621472 | tf_op jit(solution)/shard_map/all_to_all | solution.py:11
  262.2 6.7 %multiply_reduce_fusion = f32[640,1280]{1,0:T(8,128)S(1)} fusion(bf16[4,2,256,640]{3,2,1,0:T(8,128)(2,1)} %bitcast.31, bf16[4,256,1280]{2,1,0:T(8,128)(2,1)S(1)} %all-to-all-done), kind=kOutput, calls=%fused_computation | convolution fusion | flops 3367731200 | bytes 8519680 | tf_op jit(solution)/shard_map/gsti,gtj->gsij/dot_general | solution.py:40
  268.9 2.9 divide_convert_fusion
  271.8 0.0 all-gather.8.cloned.1.call-start
  271.9 2.7 constant_dynamic-slice_fusion
  274.6 0.2 reduce-scatter.5.cloned.1.call-start
  274.8 70.8 %all-gather.6.cloned.1.call-done = bf16[5120,1280]{1,0:T(8,128)(2,1)} async-done(((bf16[640,1280]{1,0:T(8,128)(2,1)}), bf16[5120,1280]{1,0:T(8,128)(2,1)}) %all-gather.6.cloned.1.call-update) | async-done | bytes 13107216 | tf_op jit(solution)/shard_map/all_gather | solution.py:48
  345.6 15.5 %convolution_convert_fusion.clone.4 = bf16[1280,640]{1,0:T(8,128)(2,1)S(1)} fusion(bf16[5120,1280]{1,0:T(8,128)(2,1)} %all-gather.6.cloned.1.call-done, bf16[640,5120]{1,0:T(8,128)(2,1)} %param.13), kind=kOutput, calls=%fused_computation.2.clone.clone.clone.1 | convolution fusion | flops 8389427200 | bytes 21299200 | tf_op jit(solution)/shard_map/dot_general | solution.py:51
  361.1 60.4 %all-gather.8.cloned.1.call-done = bf16[5120,1280]{1,0:T(8,128)(2,1)} async-done(((bf16[640,1280]{1,0:T(8,128)(2,1)}), bf16[5120,1280]{1,0:T(8,128)(2,1)}) %all-gather.8.cloned.1.call-update) | async-done | bytes 13107216 | tf_op jit(solution)/shard_map/all_gather | solution.py:49
  421.6 14.5 %fusion.1 = f32[640,5120]{1,0:T(8,128)} fusion(bf16[5120,1280]{1,0:T(8,128)(2,1)} %all-gather.8.cloned.1.call-done, bf16[1280,640]{1,0:T(8,128)(2,1)S(1)} %convolution_convert_fusion.clone.4), kind=kOutput, calls=%fused_computation.5 | convolution fusion | flops 8388608000 | bytes 27852800 | tf_op jit(solution)/shard_map/dot_general | solution.py:52
  436.1 220.5 %reduce-scatter.5.cloned.1.call-done = f32[640,1280]{1,0:T(8,128)} async-done(((f32[640,5120]{1,0:T(8,128)}), f32[640,1280]{1,0:T(8,128)}) %reduce-scatter.5.cloned.1.call-update) | async-done | bytes 3276816 | tf_op jit(solution)/shard_map/reduce_scatter | solution.py:55
  (20 shorter events, 0.1 us)
Async XLA Ops:
  7.2 1.0 copy-start
  7.2 154.3 %reduce-scatter.3.cloned.1.call-start = ((), (), s32[]{:S(2)}) async-start(), calls=%async_computation.3 | async-start | bytes 5898240 | tf_op jit(solution)/shard_map/reduce_scatter | solution.py:23
  15.5 1.0 copy-start.3
  156.3 5.1 copy-start.5
  156.3 5.1 copy-start.4
  156.3 105.9 %all-to-all-start = ((bf16[4,256,1280]{2,1,0:T(8,128)(2,1)}), bf16[4,256,1280]{2,1,0:T(8,128)(2,1)S(1)}, u32[]{:S(2)}, u32[]{:S(2)}) async-start(bf16[4,256,1280]{2,1,0:T(8,128)(2,1)} %pad_maximum_fusion), calls=%async_computation.1 | async-start | bytes 5242880 | tf_op jit(solution)/shard_map/all_to_all | solution.py:11
  161.4 100.8 %all-gather.4.cloned.1.call-start = ((), (), s32[]{:S(2)}) async-start(), calls=%async_computation.4 | async-start | bytes 3276800 | tf_op jit(solution)/shard_map/all_gather | solution.py:36
  163.7 181.9 %all-gather.6.cloned.1.call-start = ((), (), s32[]{:S(2)}) async-start(), calls=%async_computation.5 | async-start | bytes 14745600 | tf_op jit(solution)/shard_map/all_gather | solution.py:48
  262.2 6.7 %copy-start.2 = (bf16[640,1280]{1,0:T(8,128)(2,1)S(1)}, bf16[640,1280]{1,0:T(8,128)(2,1)}, u32[]{:S(2)}) copy-start(bf16[640,1280]{1,0:T(8,128)(2,1)} %param.14) | copy-start | bytes 4915204
  271.8 149.8 %all-gather.8.cloned.1.call-start = ((), (), s32[]{:S(2)}) async-start(), calls=%async_computation.6 | async-start | bytes 14745600 | tf_op jit(solution)/shard_map/all_gather | solution.py:49
  274.6 382.0 %reduce-scatter.5.cloned.1.call-start = ((), (), s32[]{:S(2)}) async-start(), calls=%async_computation.7 | async-start | bytes 16384000 | tf_op jit(solution)/shard_map/reduce_scatter | solution.py:55
  436.1 220.5 %copy-start.1 = (bf16[256,640]{1,0:T(8,128)(2,1)S(1)}, bf16[256,640]{1,0:T(8,128)(2,1)}, u32[]{:S(2)}) copy-start(bf16[256,640]{1,0:T(8,128)(2,1)} %param.9) | copy-start | bytes 983044
Sparse Core Ops, SparseCore 0:
  15.7 80.4 reduce-scatter.2
  164.3 92.1 all-gather.3
  271.9 73.6 all-gather.5
  347.3 74.1 all-gather.7
  436.2 220.3 reduce-scatter.4
